TPU v7x, 32 devices: a whole 2x2x4 slice. The times are simulated.
32 devices in a mesh: fsdp: 2 (over x), ctx: 4 (over z), tp: 4 (over y, core).
Axes of the slice: x: 2, y: 2, z: 4, core: 2. Of those that a mesh axis runs over, the one named last changes fastest.
Arguments:
- inputs: bfloat16 [2, 1024, 2048], P('fsdp', 'ctx'), may hold values from -6 to 6
- attn_gain: bfloat16 [2048], P(('fsdp', 'ctx')), may hold values from 0.099609375 to 1.8984375
- qkv_weight: bfloat16 [2048, 3, 2048], P(('fsdp', 'ctx'), None, 'tp'), may hold values from -0.125 to 0.125
- out_weight: bfloat16 [2048, 2048], P(('fsdp', 'ctx'), 'tp'), may hold values from -1 to 1
- qk_gains: bfloat16 [2, 2048], P(None, 'tp'), may hold values from 0.099609375 to 1.8984375
- mlp_gain: bfloat16 [2048], P(('fsdp', 'ctx')), may hold values from 0.099609375 to 1.8984375
- router_weight: bfloat16 [2048, 8], P(('fsdp', 'ctx')), may hold values from -0.0625 to 0.0625
- gate_up_weight: bfloat16 [2048, 2, 8, 1024], P(('fsdp', 'ctx'), None, None, 'tp'), may hold values from -0.125 to 0.125
- down_weight: bfloat16 [2048, 8, 1024], P(('fsdp', 'ctx'), None, 'tp'), may hold values from -1.5 to 1.5
- routes: int32 [4, 2, 256, 4], P('ctx', 'fsdp'), may hold values from 0 to 7, all different within a row; in each aligned block of 256 rows (0 to 255, 256 to 511, ..., all dimensions but the last counted through in order) at most 160 rows name the same one
- cotangent: bfloat16 [2, 1024, 2048], P('fsdp', 'ctx'), may hold values from -6 to 6
Outputs:
- output: bfloat16 [2, 1024, 2048], P('fsdp', 'ctx')
- grad_inputs: float32 [2, 1024, 2048], P('fsdp', 'ctx')
- grad_attn_gain: float32 [2048], P(('fsdp', 'ctx'))
- grad_qkv: float32 [2048, 3, 2048], P(('fsdp', 'ctx'), None, 'tp')
- grad_out: float32 [2048, 2048], P(('fsdp', 'ctx'), 'tp')
- grad_qk_gains: float32 [2, 2048], P(None, 'tp')
- grad_mlp_gain: float32 [2048], P(('fsdp', 'ctx'))
- grad_router: float32 [2048, 8], P(('fsdp', 'ctx'))
- grad_gate_up: float32 [2048, 2, 8, 1024], P(('fsdp', 'ctx'), None, None, 'tp')
- grad_down: float32 [2048, 8, 1024], P(('fsdp', 'ctx'), None, 'tp')
Inputs may be any that keep to these rules, and one draw needn't show every extreme that they name: `routes`: each row names 4 different experts. Among the 256 tokens of one device (aligned blocks of the array in its order) no expert is named more than 160 times, a bound that some block reaches.
All inputs are finite; a program needn't handle non-finite values.
Results may differ from a plain program's by a relative error of at most 0.017.
Values may be sent and summed in bfloat16 or wider, within the bound.
A program may use at most 256 MiB of HBM per device.

v0:
```python
import math
import jax
import jax.numpy as jnp
from jax import lax
from jax.sharding import PartitionSpec as P

HEAD_DIM = 128
TOPK = 4
EXPERTS = 8
HQ = 2048
CAP = 160
epsilon = 1e-05
highest = lax.Precision.HIGHEST


def inv_rms(values):
    return lax.rsqrt(jnp.mean(values * values, axis=-1, keepdims=True) + epsilon)


def rotary_tables(offset, length):
    half_dim = HEAD_DIM // 2
    frequency = jnp.exp(
        jnp.arange(half_dim, dtype=jnp.float32) * (-2.0 * math.log(10000.0) / HEAD_DIM)
    )
    positions = (offset + jnp.arange(length, dtype=jnp.int32)).astype(jnp.float32)
    angles = positions[:, None] * frequency[None, :]
    angles = jnp.concatenate([angles, angles], axis=1)
    return (jnp.cos(angles), jnp.sin(angles))


def rotate(values, cosine, sine_table):
    half_dim = values.shape[-1] // 2
    turned = jnp.concatenate([-values[..., half_dim:], values[..., :half_dim]], axis=-1)
    return values * cosine + turned * sine_table


def rotate_back(grads, cosine, sine_table):
    half_dim = grads.shape[-1] // 2
    scaled = grads * sine_table
    return grads * cosine + jnp.concatenate(
        [scaled[..., half_dim:], -scaled[..., :half_dim]], axis=-1
    )


def slot_table(routed):
    flat_routes = routed.reshape(-1)
    one_hot = (flat_routes[:, None] == jnp.arange(EXPERTS, dtype=jnp.int32)[None, :]).astype(
        jnp.int32
    )
    earlier = jnp.cumsum(one_hot, axis=0) - one_hot
    within = jnp.sum(earlier * one_hot, axis=1)
    slots = flat_routes * CAP + within
    owners = jnp.arange(flat_routes.shape[0], dtype=jnp.int32) // TOPK
    token_of = jnp.zeros((EXPERTS * CAP,), jnp.int32).at[slots].set(owners)
    filled = jnp.zeros((EXPERTS * CAP,), jnp.float32).at[slots].set(1.0)
    return (slots.reshape(routed.shape), token_of, filled)


def on_device(
    inputs,
    attn_gain,
    qkv_weight,
    out_weight,
    qk_gains,
    mlp_gain,
    router_weight,
    gate_up_weight,
    down_weight,
    routes,
    cotangent,
):
    seq_dev, block, width = inputs.shape
    rows = seq_dev * block
    heads_dev = qkv_weight.shape[2] // HEAD_DIM
    scale = 1.0 / math.sqrt(HEAD_DIM)
    place = lax.axis_index("ctx")
    attn_gain_all, qkv_all, out_all, mlp_gain_all, router_all = (
        lax.all_gather(attn_gain, ("fsdp", "ctx"), axis=0, tiled=True),
        lax.all_gather(qkv_weight, ("fsdp", "ctx"), axis=0, tiled=True),
        lax.all_gather(out_weight, ("fsdp", "ctx"), axis=0, tiled=True),
        lax.all_gather(mlp_gain, ("fsdp", "ctx"), axis=0, tiled=True),
        lax.all_gather(router_weight, ("fsdp", "ctx"), axis=0, tiled=True),
    )
    attn_scale = attn_gain_all.astype(jnp.float32)
    mlp_scale = mlp_gain_all.astype(jnp.float32)
    flat_in = inputs.reshape(rows, width).astype(jnp.float32)
    first_rms = inv_rms(flat_in)
    normed = (flat_in * first_rms * attn_scale).astype(jnp.bfloat16)
    projected = jnp.einsum("td,dch->tch", normed, qkv_all, preferred_element_type=jnp.float32)
    query_proj = projected[:, 0]
    key_proj = projected[:, 1]
    query_sums, key_sums = lax.psum(
        (jnp.sum(query_proj * query_proj, axis=-1), jnp.sum(key_proj * key_proj, axis=-1)), "tp"
    )
    query_rms = lax.rsqrt(query_sums / HQ + epsilon)[:, None]
    key_rms = lax.rsqrt(key_sums / HQ + epsilon)[:, None]
    query_gain = qk_gains[0].astype(jnp.float32)
    key_gain = qk_gains[1].astype(jnp.float32)
    query_norm = query_proj * query_rms * query_gain
    key_norm = key_proj * key_rms * key_gain
    cosine, sine_table = rotary_tables(place * block, block)
    cos_heads = cosine[:, None, :]
    sin_heads = sine_table[:, None, :]
    head_shape = (seq_dev, block, heads_dev, HEAD_DIM)
    query_rot = rotate(query_norm.reshape(head_shape), cos_heads, sin_heads).astype(jnp.bfloat16)
    key_rot = rotate(key_norm.reshape(head_shape), cos_heads, sin_heads).astype(jnp.bfloat16)
    value_heads = projected[:, 2].reshape(head_shape).astype(jnp.bfloat16)
    key_all, value_all = (
        lax.all_gather(key_rot, "ctx", axis=1, tiled=True),
        lax.all_gather(value_heads, "ctx", axis=1, tiled=True),
    )
    length = key_all.shape[1]
    key_block = jnp.arange(length, dtype=jnp.int32) // block
    allowed = (key_block <= place)[None, None, None, :]
    scores = (
        jnp.einsum("sqhd,skhd->shqk", query_rot, key_all, preferred_element_type=jnp.float32)
        * scale
    )
    scores = jnp.where(allowed, scores, -1e30)
    top_score = jnp.max(scores, axis=-1, keepdims=True)
    exponent = jnp.exp(scores - top_score)
    total = jnp.sum(exponent, axis=-1, keepdims=True)
    log_total = top_score + jnp.log(total)
    softmaxed = exponent / total
    attended = jnp.einsum(
        "shqk,skhd->sqhd",
        softmaxed.astype(jnp.bfloat16),
        value_all,
        preferred_element_type=jnp.float32,
    )
    attended = attended.reshape(rows, heads_dev * HEAD_DIM).astype(jnp.bfloat16)
    branch = lax.psum(
        jnp.einsum("th,dh->td", attended, out_all, preferred_element_type=jnp.float32), "tp"
    )
    middle = flat_in + branch
    second_rms = inv_rms(middle)
    normed_mlp = (middle * second_rms * mlp_scale).astype(jnp.bfloat16)
    logits = jnp.dot(normed_mlp, router_all, preferred_element_type=jnp.float32)
    chances = jax.nn.softmax(logits, axis=-1)
    routed = routes.reshape(rows, TOPK)
    gates = jnp.take_along_axis(chances, routed, axis=-1)
    slots, token_of, filled = slot_table(routed)
    dispatched = (normed_mlp[token_of] * filled[:, None].astype(jnp.bfloat16)).reshape(
        EXPERTS, CAP, width
    )
    gate_up_all, down_all = (
        lax.all_gather(gate_up_weight, ("fsdp", "ctx"), axis=0, tiled=True),
        lax.all_gather(down_weight, ("fsdp", "ctx"), axis=0, tiled=True),
    )
    gate_up = jnp.einsum(
        "ecd,djef->ecjf", dispatched, gate_up_all, preferred_element_type=jnp.float32
    )
    gate_part = gate_up[:, :, 0]
    up_part = gate_up[:, :, 1]
    activated = (jax.nn.silu(gate_part) * up_part).astype(jnp.bfloat16)
    upstream = cotangent.reshape(rows, width).astype(jnp.float32)
    slot_gates = (
        jnp.zeros((EXPERTS * CAP,), jnp.float32)
        .at[slots.reshape(-1)]
        .set(gates.reshape(-1))
        .reshape(EXPERTS, CAP)
    )
    token_grid = token_of.reshape(EXPERTS, CAP)
    filled_grid = filled.reshape(EXPERTS, CAP)

    def expert_forward(expert_index, running):
        combined, slot_products = running
        expert_down = lax.dynamic_index_in_dim(down_all, expert_index, 1, keepdims=False)
        expert_act = lax.dynamic_index_in_dim(activated, expert_index, 0, keepdims=False)
        expert_tokens = lax.dynamic_index_in_dim(token_grid, expert_index, 0, keepdims=False)
        expert_gates = lax.dynamic_index_in_dim(slot_gates, expert_index, 0, keepdims=False)
        returned_rows = jnp.einsum(
            "cf,df->cd", expert_act, expert_down, preferred_element_type=jnp.float32
        )
        combined = combined.at[expert_tokens].add(returned_rows * expert_gates[:, None])
        products = jnp.sum(returned_rows * upstream[expert_tokens], axis=-1)
        slot_products = lax.dynamic_update_index_in_dim(slot_products, products, expert_index, 0)
        return (combined, slot_products)

    combined, slot_products = lax.fori_loop(
        0,
        EXPERTS,
        expert_forward,
        (jnp.zeros((rows, width), jnp.float32), jnp.zeros((EXPERTS, CAP), jnp.float32)),
    )
    gate_grad_part = slot_products.reshape(-1)[slots]
    expert_sum = lax.psum(combined, "tp")
    output = (middle + expert_sum).astype(jnp.bfloat16).reshape(seq_dev, block, width)
    slot_grads = (
        (slot_gates.reshape(-1)[:, None] * upstream[token_of])
        .astype(jnp.bfloat16)
        .reshape(EXPERTS, CAP, width)
    )
    gate_up_back, down_back = (
        lax.all_gather(gate_up_weight, ("fsdp", "ctx"), axis=0, tiled=True),
        lax.all_gather(down_weight, ("fsdp", "ctx"), axis=0, tiled=True),
    )
    act_grads = jnp.einsum(
        "ecd,def->ecf", slot_grads, down_back, preferred_element_type=jnp.float32
    )
    sigmoid = jax.nn.sigmoid(gate_part)
    gate_grads = act_grads * up_part * sigmoid * (1.0 + gate_part * (1.0 - sigmoid))
    up_grads = act_grads * (gate_part * sigmoid)
    pre_grads = jnp.stack([gate_grads, up_grads], axis=2).astype(jnp.bfloat16)

    def expert_backward(expert_index, running):
        expert_pre = lax.dynamic_index_in_dim(pre_grads, expert_index, 0, keepdims=False)
        expert_weight = lax.dynamic_index_in_dim(gate_up_back, expert_index, 2, keepdims=False)
        expert_tokens = lax.dynamic_index_in_dim(token_grid, expert_index, 0, keepdims=False)
        expert_filled = lax.dynamic_index_in_dim(filled_grid, expert_index, 0, keepdims=False)
        expert_back = jnp.einsum(
            "cjf,djf->cd", expert_pre, expert_weight, preferred_element_type=jnp.float32
        )
        return running.at[expert_tokens].add(expert_back * expert_filled[:, None])

    expert_input_part = lax.fori_loop(
        0, EXPERTS, expert_backward, jnp.zeros((rows, width), jnp.float32)
    )
    gate_up_term = jnp.einsum(
        "ecd,ecjf->djef", dispatched, pre_grads, preferred_element_type=jnp.float32
    )
    down_term = jnp.einsum(
        "ecf,ecd->def", activated, slot_grads, preferred_element_type=jnp.float32
    )
    expert_grads = lax.psum_scatter(
        jnp.concatenate([gate_up_term, down_term[:, None]], axis=1),
        ("fsdp", "ctx"),
        scatter_dimension=0,
        tiled=True,
    )
    gate_up_share = expert_grads[:, :2]
    down_share = expert_grads[:, 2]
    expert_input, gate_total = lax.psum((expert_input_part, gate_grad_part), "tp")
    chosen = (routed[:, :, None] == jnp.arange(EXPERTS, dtype=jnp.int32)[None, None, :]).astype(
        jnp.float32
    )
    chance_grads = jnp.sum(gate_total[:, :, None] * chosen, axis=1)
    logit_grads = chances * (chance_grads - jnp.sum(chances * chance_grads, axis=-1, keepdims=True))
    router_f32 = router_all.astype(jnp.float32)
    mlp_input = expert_input + jnp.dot(logit_grads, router_f32.T, precision=highest)
    grad_router = jnp.dot(normed_mlp.astype(jnp.float32).T, logit_grads, precision=highest)
    grad_mlp_gain = jnp.sum(mlp_input * middle * second_rms, axis=0)
    scaled_mlp = mlp_input * mlp_scale
    middle_grad = (
        upstream
        + second_rms * scaled_mlp
        - middle * second_rms**3 / width * jnp.sum(scaled_mlp * middle, axis=-1, keepdims=True)
    )
    branch_grad = middle_grad.astype(jnp.bfloat16)
    grad_out = jnp.einsum("td,th->dh", branch_grad, attended, preferred_element_type=jnp.float32)
    attended_grad = (
        jnp.dot(branch_grad, out_all, preferred_element_type=jnp.float32)
        .astype(jnp.bfloat16)
        .reshape(head_shape)
    )
    again_scores = (
        jnp.einsum("sqhd,skhd->shqk", query_rot, key_all, preferred_element_type=jnp.float32)
        * scale
    )
    again_scores = jnp.where(allowed, again_scores, -1e30)
    recomputed = jnp.exp(again_scores - log_total)
    prob_grads = jnp.einsum(
        "sqhd,skhd->shqk", attended_grad, value_all, preferred_element_type=jnp.float32
    )
    score_grads = (
        recomputed * (prob_grads - jnp.sum(recomputed * prob_grads, axis=-1, keepdims=True))
    ).astype(jnp.bfloat16)
    query_grads = (
        jnp.einsum("shqk,skhd->sqhd", score_grads, key_all, preferred_element_type=jnp.float32)
        * scale
    )
    key_grads = (
        jnp.einsum("shqk,sqhd->skhd", score_grads, query_rot, preferred_element_type=jnp.float32)
        * scale
    )
    value_grads = jnp.einsum(
        "shqk,sqhd->skhd",
        recomputed.astype(jnp.bfloat16),
        attended_grad,
        preferred_element_type=jnp.float32,
    )
    key_back, value_back = (
        lax.psum_scatter(key_grads, "ctx", scatter_dimension=1, tiled=True),
        lax.psum_scatter(value_grads, "ctx", scatter_dimension=1, tiled=True),
    )
    query_norm_grad = rotate_back(query_grads, cos_heads, sin_heads).reshape(rows, -1)
    key_norm_grad = rotate_back(key_back, cos_heads, sin_heads).reshape(rows, -1)
    query_scaled = query_norm_grad * query_gain
    key_scaled = key_norm_grad * key_gain
    query_inner, key_inner = lax.psum(
        (jnp.sum(query_scaled * query_proj, axis=-1), jnp.sum(key_scaled * key_proj, axis=-1)), "tp"
    )
    query_pre = query_rms * query_scaled - query_proj * query_rms**3 / HQ * query_inner[:, None]
    key_pre = key_rms * key_scaled - key_proj * key_rms**3 / HQ * key_inner[:, None]
    gain_terms = jnp.stack(
        [
            jnp.sum(query_norm_grad * query_proj * query_rms, axis=0),
            jnp.sum(key_norm_grad * key_proj * key_rms, axis=0),
        ]
    )
    grad_qk_gains = lax.psum(gain_terms, ("fsdp", "ctx"))
    proj_grads = jnp.stack([query_pre, key_pre, value_back.reshape(rows, -1)], axis=1).astype(
        jnp.bfloat16
    )
    grad_qkv = jnp.einsum("td,tch->dch", normed, proj_grads, preferred_element_type=jnp.float32)
    normed_grad = lax.psum(
        jnp.einsum("tch,dch->td", proj_grads, qkv_all, preferred_element_type=jnp.float32), "tp"
    )
    grad_attn_gain = jnp.sum(normed_grad * flat_in * first_rms, axis=0)
    scaled_first = normed_grad * attn_scale
    grad_inputs = (
        middle_grad
        + first_rms * scaled_first
        - flat_in * first_rms**3 / width * jnp.sum(scaled_first * flat_in, axis=-1, keepdims=True)
    )
    shares = (
        lax.psum_scatter(grad_attn_gain, ("fsdp", "ctx"), scatter_dimension=0, tiled=True),
        lax.psum_scatter(grad_qkv, ("fsdp", "ctx"), scatter_dimension=0, tiled=True),
        lax.psum_scatter(grad_out, ("fsdp", "ctx"), scatter_dimension=0, tiled=True),
        lax.psum_scatter(grad_mlp_gain, ("fsdp", "ctx"), scatter_dimension=0, tiled=True),
        lax.psum_scatter(grad_router, ("fsdp", "ctx"), scatter_dimension=0, tiled=True),
    )
    return (
        output,
        grad_inputs.reshape(seq_dev, block, width),
        shares[0],
        shares[1],
        shares[2],
        grad_qk_gains,
        shares[3],
        shares[4],
        gate_up_share,
        down_share,
    )


def solution(mesh):
    placed = (
        P("fsdp", "ctx", None),
        P(("fsdp", "ctx")),
        P(("fsdp", "ctx"), None, "tp"),
        P(("fsdp", "ctx"), "tp"),
        P(None, "tp"),
        P(("fsdp", "ctx")),
        P(("fsdp", "ctx"), None),
        P(("fsdp", "ctx"), None, None, "tp"),
        P(("fsdp", "ctx"), None, "tp"),
        P("ctx", "fsdp", None, None),
        P("fsdp", "ctx", None),
    )
    return jax.shard_map(
        on_device,
        mesh=mesh,
        in_specs=placed,
        out_specs=(
            P("fsdp", "ctx", None),
            P("fsdp", "ctx", None),
            P(("fsdp", "ctx")),
            P(("fsdp", "ctx"), None, "tp"),
            P(("fsdp", "ctx"), "tp"),
            P(None, "tp"),
            P(("fsdp", "ctx")),
            P(("fsdp", "ctx"), None),
            P(("fsdp", "ctx"), None, None, "tp"),
            P(("fsdp", "ctx"), None, "tp"),
        ),
        check_vma=False,
    )
```

profile of v0, /device:TPU:0, one launch (start us, length us, event | category | flops | bytes accessed | tf_op | source)
XLA Modules:
  0.0 2206.6 jit_solution(5604651613465843333)
XLA Ops:
  8.6 22.6 %all-gather = bf16[8,1,256]{2,1,0:T(2,128)(2,1)S(1)} all-gather(bf16[1,1,256]{2,1,0:T(2,128)(2,1)S(1)} %reshape.832), channel_id=1, replica_groups=mesh['fsdp'=2,'ctx'=4,'tp'=4] {'fsdp','ctx'}, dimensions={0}, use_global_device_ids=true | all-gather | bytes 4608 | tf_op jit(solution)/shard_map/all_gather | solution.py:78
  33.5 78.4 %all-gather.9.cloned.1.call-done = bf16[2048,3,512]{2,0,1:T(8,128)(2,1)} async-done(((bf16[256,3,512]{2,0,1:T(8,128)(2,1)}), bf16[2048,3,512]{2,0,1:T(8,128)(2,1)}) %all-gather.9.cloned.1.call-update) | async-done | bytes 6291472 | tf_op jit(solution)/shard_map/all_gather | solution.py:79
  131.8 21.5 all-gather.13.cloned.1.call-done
  158.5 26.7 %all-gather.11.cloned.1.call-done = bf16[1,1024,4,128]{1,3,2,0:T(8,128)(2,1)} async-done(((bf16[1,256,4,128]{1,3,2,0:T(8,128)(2,1)}), bf16[1,1024,4,128]{1,3,2,0:T(8,128)(2,1)}) %all-gather.11.cloned.1.call-update) | async-done | bytes 1048592 | tf_op jit(solution)/shard_map/all_gather | solution.py:110
  188.7 46.1 %all-gather.15.cloned.1.call-done = bf16[2048,512]{1,0:T(8,128)(2,1)} async-done(((bf16[256,512]{1,0:T(8,128)(2,1)}), bf16[2048,512]{1,0:T(8,128)(2,1)}) %all-gather.15.cloned.1.call-update) | async-done | bytes 2097168 | tf_op jit(solution)/shard_map/all_gather | solution.py:80
  252.7 18.0 all-gather.1
  284.5 30.8 %all_gather.37 = bf16[2048,8]{0,1:T(8,128)(2,1)S(1)} all-gather(bf16[256,8]{0,1:T(8,128)(2,1)S(1)} %copy-done.73), channel_id=1, replica_groups=mesh['fsdp'=2,'ctx'=4,'tp'=4] {'fsdp','ctx'}, dimensions={0}, use_global_device_ids=true | all-gather | bytes 36864 | tf_op jit(solution)/shard_map/all_gather | solution.py:82
  337.1 182.0 %all-gather.17.cloned.1.call-done = bf16[2048,2,8,256]{3,0,1,2:T(8,128)(2,1)} async-done(((bf16[256,2,8,256]{3,0,1,2:T(8,128)(2,1)}), bf16[2048,2,8,256]{3,0,1,2:T(8,128)(2,1)}) %all-gather.17.cloned.1.call-update) | async-done | bytes 16777232 | tf_op jit(solution)/shard_map/all_gather | solution.py:147
  519.1 11.7 fusion.16
  530.8 114.3 %all-gather.19.cloned.1.call-done = bf16[2048,8,256]{2,0,1:T(8,128)(2,1)} async-done(((bf16[256,8,256]{2,0,1:T(8,128)(2,1)}), bf16[2048,8,256]{2,0,1:T(8,128)(2,1)}) %all-gather.19.cloned.1.call-update) | async-done | bytes 8388624 | tf_op jit(solution)/shard_map/all_gather | solution.py:148
  645.2 10.0 fusion.51
  658.3 63.9 %while.29 = (s32[]{:T(128)}, f32[256,2048]{1,0:T(8,128)}, s32[8,160]{1,0:T(8,128)S(1)}, bf16[8,160,2,256]{3,1,2,0:T(8,128)(2,1)}, bf16[2048,2,8,256]{3,0,1,2:T(8,128)(2,1)}, /*index=5*/f32[8,160]{1,0:T(8,128)S(1)}, s32[]{:T(128)}) while((s32[]{:T(128)}, f32[256,2048]{1,0:T(8,128)}, s32[8,160]{1,0:T(8,128)S(1)}, ...), condition=%wide.region_24.25_spmd, body=%wide.region_22.24_spmd.sunk | while | flops 336200160 | bytes 7508829 | solution.py:216
  723.8 80.3 %while.28 = (s32[]{:T(128)}, f32[256,2048]{1,0:T(8,128)}, f32[8,160]{1,0:T(8,128)S(1)}, s32[8,160]{1,0:T(8,128)S(1)}, bf16[8,160,256]{2,1,0:T(8,128)(2,1)}, /*in...) while((s32[]{:T(128)}, f32[256,2048]{1,0:T(8,128)}, ...), condition=%wide.region_20.21_spmd, body=%wide.region_17.20_spmd.sunk | while | flops 169084224 | bytes 9793273 | solution.py:180
  810.5 25.5 %psum.75 = f32[256,4]{1,0:T(8,128)S(1)} all-reduce(f32[256,4]{1,0:T(8,128)S(1)} %reshape.775), channel_id=1, replica_groups=mesh['fsdp'=2,'ctx'=4,'tp'=4] {'tp'}, use_global_device_ids=true, to_apply=%region_26.27 | all-reduce | flops 1024 | bytes 8192 | tf_op jit(solution)/shard_map/psum | solution.py:233
  856.5 18.8 convolution_bitcast_fusion.1
  890.5 43.5 %reduce-scatter.7.cloned.1.call-done = f32[1,256,4,128]{3,1,2,0:T(8,128)} async-done(((f32[1,1024,4,128]{3,1,2,0:T(8,128)}), f32[1,256,4,128]{3,1,2,0:T(8,128)}) %reduce-scatter.7.cloned.1.call-update) | async-done | bytes 524304 | tf_op jit(solution)/shard_map/reduce_scatter | solution.py:283
  954.0 12.9 convolution_bitcast_fusion.2
  966.9 33.6 %pad_maximum_fusion = f32[2048,3,8,256]{0,3,1,2:T(8,128)} fusion(f32[2048,1,8,256]{0,3,1,2:T(8,128)} %convolution_bitcast_fusion.2, f32[2048,2,8,256]{0,3,1,2:T(8,128)} %convolution_bitcast_fusion.1), kind=kLoop, calls=%fused_computation.32 | loop fusion | flops 12582912 | bytes 100663296 | tf_op jit(solution)/shard_map/concatenate | solution.py:226
  1018.2 19.5 all-reduce.14.cloned.1.call-done
  1039.8 38.9 %all-reduce.2 = (f32[2048]{0:T(1024)S(1)}, f32[2,512]{1,0:T(2,128)}, f32[2048]{0:T(1024)S(1)}) all-reduce(f32[2048]{0:T(1024)S(1)} %get-tuple-element.336, f32[2,512]{1,0:T(2,128)S(1)} %pad_maximum_fusion.6, f32[2048]{0:T(1024)S(1)} %get-tuple-element.334), channel_id=4, replica_groups=mesh['fsdp'=2,'ctx'=4,'tp'=4] {'fsdp','ctx'}, use_global_device_ids=true, to_apply=%region_40.41.clone | all-reduce | flops 5120 | bytes 40960
  1085.0 747.3 %reduce-scatter.17.cloned.1.call-done = f32[256,3,8,256]{0,3,1,2:T(8,128)} async-done(((f32[2048,3,8,256]{0,3,1,2:T(8,128)}), f32[256,3,8,256]{0,3,1,2:T(8,128)}) %reduce-scatter.17.cloned.1.call-update) | async-done | bytes 6291472 | tf_op jit(solution)/shard_map/reduce_scatter | solution.py:225
  1846.1 50.5 %reduce-scatter.15.cloned.1.call-done = f32[256,8]{0,1:T(8,128)} async-done(((f32[2048,8]{0,1:T(8,128)}), f32[256,8]{0,1:T(8,128)}) %reduce-scatter.15.cloned.1.call-update) | async-done | bytes 8208 | tf_op jit(solution)/shard_map/reduce_scatter | solution.py:321
  1896.6 91.0 %reduce-scatter.13.cloned.1.call-done = f32[256,512]{1,0:T(8,128)} async-done(((f32[2048,512]{1,0:T(8,128)}), f32[256,512]{1,0:T(8,128)}) %reduce-scatter.13.cloned.1.call-update) | async-done | bytes 524304 | tf_op jit(solution)/shard_map/reduce_scatter | solution.py:319
  1987.7 212.1 %reduce-scatter.11.cloned.1.call-done = f32[256,3,512]{2,0,1:T(8,128)} async-done(((f32[2048,3,512]{2,0,1:T(8,128)}), f32[256,3,512]{2,0,1:T(8,128)}) %reduce-scatter.11.cloned.1.call-update) | async-done | bytes 1572880 | tf_op jit(solution)/shard_map/reduce_scatter | solution.py:318
  (405 shorter events, 334.6 us)
Async XLA Ops:
  7.2 104.8 %all-gather.9.cloned.1.call-start = ((), (), s32[]{:S(2)}) async-start(), calls=%async_computation.6 | async-start | bytes 7077888 | tf_op jit(solution)/shard_map/all_gather | solution.py:79
  7.9 145.3 %all-gather.13.cloned.1.call-start = ((), (), s32[]{:S(2)}) async-start(), calls=%async_computation.8 | async-start | bytes 1310720 | tf_op jit(solution)/shard_map/all_gather | solution.py:109
  31.2 85.3 %copy-start.43 = (f32[8,1,256]{2,1,0:T(1,128)}, f32[8,1,256]{2,1,0:T(1,128)S(1)}, u32[]{:S(2)}) copy-start(f32[8,1,256]{2,1,0:T(1,128)S(1)} %convert_element_type.162) | copy-start | bytes 24580
  32.7 97.7 %copy-start.28 = (f32[256,128]{1,0:T(8,128)}, f32[256,128]{1,0:T(8,128)S(1)}, u32[]{:S(2)}) copy-start(f32[256,128]{1,0:T(8,128)S(1)} %get-tuple-element.404) | copy-start | bytes 393220
  32.7 97.8 %copy-start.26 = (f32[256,128]{1,0:T(8,128)}, f32[256,128]{1,0:T(8,128)S(1)}, u32[]{:S(2)}) copy-start(f32[256,128]{1,0:T(8,128)S(1)} %get-tuple-element.405) | copy-start | bytes 393220
  33.5 83.1 %copy-start.60 = (f32[256]{0:T(256)}, f32[256]{0:T(256)S(1)}, u32[]{:S(2)}) copy-start(f32[256]{0:T(256)S(1)} %get-tuple-element.411) | copy-start | bytes 3076
  33.5 92.6 %copy-start.50 = (f32[1,512]{1,0:T(1,128)}, f32[1,512]{1,0:T(1,128)S(1)}, u32[]{:S(2)}) copy-start(f32[1,512]{1,0:T(1,128)S(1)} %get-tuple-element.408) | copy-start | bytes 6148
  33.5 98.1 %copy-start.52 = (f32[1,512]{1,0:T(1,128)}, f32[1,512]{1,0:T(1,128)S(1)}, u32[]{:S(2)}) copy-start(f32[1,512]{1,0:T(1,128)S(1)} %get-tuple-element.409) | copy-start | bytes 6148
  127.1 58.0 %all-gather.11.cloned.1.call-start = ((), (), s32[]{:S(2)}) async-start(), calls=%async_computation.7 | async-start | bytes 1310720 | tf_op jit(solution)/shard_map/all_gather | solution.py:110
  129.7 105.0 %all-gather.15.cloned.1.call-start = ((), (), s32[]{:S(2)}) async-start(), calls=%async_computation.9 | async-start | bytes 2359296 | tf_op jit(solution)/shard_map/all_gather | solution.py:80
  130.3 185.7 %all-reduce.10.cloned.1.call-start = ((), (), s32[]{:S(2)}) async-start(), calls=%async_computation.10 | async-start | bytes 4194304 | tf_op jit(solution)/shard_map/psum | solution.py:132
  188.7 46.1 %copy-start.37 = (bf16[4,128,256]{2,1,0:T(8,128)(2,1)}, bf16[4,128,256]{2,1,0:T(8,128)(2,1)S(1)}, u32[]{:S(2)}) copy-start(bf16[4,128,256]{2,1,0:T(8,128)(2,1)S(1)} %fusion.42) | copy-start | bytes 786436
  238.5 280.7 %all-gather.17.cloned.1.call-start = ((), (), s32[]{:S(2)}) async-start(), calls=%async_computation.11 | async-start | bytes 18874368 | tf_op jit(solution)/shard_map/all_gather | solution.py:147
  242.1 403.1 %all-gather.19.cloned.1.call-start = ((), (), s32[]{:S(2)}) async-start(), calls=%async_computation.12 | async-start | bytes 9437184 | tf_op jit(solution)/shard_map/all_gather | solution.py:148
  244.6 591.7 %all-reduce.12.cloned.1.call-start = ((), (), s32[]{:S(2)}) async-start(), calls=%async_computation.13 | async-start | bytes 4194304 | tf_op jit(solution)/shard_map/psum | solution.py:233
  270.7 47.9 %copy-start.45 = (f32[8,1,256]{2,1,0:T(1,128)}, f32[8,1,256]{2,1,0:T(1,128)S(1)}, u32[]{:S(2)}) copy-start(f32[8,1,256]{2,1,0:T(1,128)S(1)} %convert_element_type.163) | copy-start | bytes 24580
  722.2 166.4 %reduce-scatter.9.cloned.1.call-start = ((), (), s32[]{:S(2)}) async-start(), calls=%async_computation.15 | async-start | bytes 2621440 | tf_op jit(solution)/shard_map/reduce_scatter | solution.py:284
  846.9 87.2 %reduce-scatter.7.cloned.1.call-start = ((), (), s32[]{:S(2)}) async-start(), calls=%async_computation.14 | async-start | bytes 2621440 | tf_op jit(solution)/shard_map/reduce_scatter | solution.py:283
  855.3 182.4 %all-reduce.14.cloned.1.call-start = ((), (), s32[]{:S(2)}) async-start(), calls=%async_computation.20 | async-start | bytes 8388608 | tf_op jit(solution)/shard_map/psum | solution.py:187
  876.6 57.4 %copy-start.29 = (f32[256,128]{1,0:T(8,128)S(1)}, f32[256,128]{1,0:T(8,128)}, u32[]{:S(2)}) copy-start(f32[256,128]{1,0:T(8,128)} %copy-done.28) | copy-start | bytes 393220
  953.0 879.3 %reduce-scatter.17.cloned.1.call-start = ((), (), s32[]{:S(2)}) async-start(), calls=%async_computation.19 | async-start | bytes 56623104 | tf_op jit(solution)/shard_map/reduce_scatter | solution.py:225
  1000.6 896.1 %reduce-scatter.15.cloned.1.call-start = ((), (), s32[]{:S(2)}) async-start(), calls=%async_computation.18 | async-start | bytes 73728 | tf_op jit(solution)/shard_map/reduce_scatter | solution.py:321
  1003.1 984.6 %reduce-scatter.13.cloned.1.call-start = ((), (), s32[]{:S(2)}) async-start(), calls=%async_computation.17 | async-start | bytes 4718592 | tf_op jit(solution)/shard_map/reduce_scatter | solution.py:319
  1007.7 1192.1 %reduce-scatter.11.cloned.1.call-start = ((), (), s32[]{:S(2)}) async-start(), calls=%async_computation.16 | async-start | bytes 14155776 | tf_op jit(solution)/shard_map/reduce_scatter | solution.py:318
  (67 other events, 724.0 us)
Sparse Core Ops, SparseCore 0:
  10.2 101.7 all-gather.8
  127.2 25.9 all-gather.12
  155.4 29.6 all-gather.10
  187.1 47.5 all-gather.14
  238.6 49.8 all-reduce.9
  291.3 227.7 all-gather.16
  522.0 123.1 all-gather.18
  722.3 49.5 all-reduce.11
  847.0 41.5 reduce-scatter.8
  890.8 43.1 reduce-scatter.6
  953.1 84.5 all-reduce.13
  1041.9 790.2 reduce-scatter.16
  1836.2 60.3 reduce-scatter.14
  1900.7 86.9 reduce-scatter.12
  1992.1 207.5 reduce-scatter.10
where the time goes:
time: 2220 us; the launch traced here: 2210 us
  waiting for transfers between devices  1640 us (74%)
  other arithmetic  150 us (7%)
  blocking collectives  148 us (7%)
  matrix products  141 us (6%)
  local copies, waits for them, and re-layouts  106 us (5%)
    reduce_scatter x1, waiting for transfers between devices, on_device(): lax.psum_scatter(jnp.concatenate([gate_up_term, down_term[:, None]], axis...  747 us
    reduce_scatter x1, waiting for transfers between devices, on_device(): lax.psum_scatter(grad_qkv, ('fsdp', 'ctx'), scatter_dimension=0, tiled=True)  212 us
    all_gather x1, waiting for transfers between devices, on_device(): lax.all_gather(gate_up_weight, ('fsdp', 'ctx'), axis=0, tiled=True)  182 us
    all_gather x1, waiting for transfers between devices, on_device(): lax.all_gather(down_weight, ('fsdp', 'ctx'), axis=0, tiled=True)  114 us
    reduce_scatter x1, waiting for transfers between devices, on_device(): lax.psum_scatter(grad_out, ('fsdp', 'ctx'), scatter_dimension=0, tiled=True)  91 us
    all_gather x1, waiting for transfers between devices, on_device(): lax.all_gather(qkv_weight, ('fsdp', 'ctx'), axis=0, tiled=True)  78.4 us
    reduce_scatter x1, waiting for transfers between devices, on_device(): lax.psum_scatter(grad_router, ('fsdp', 'ctx'), scatter_dimension=0, tiled...  50.5 us
    all_gather x1, waiting for transfers between devices, on_device(): lax.all_gather(out_weight, ('fsdp', 'ctx'), axis=0, tiled=True)  46.1 us
  transfers between devices with their start and end apart: 15, of which 13 were waited for; matrix products, arithmetic and copies ran while one was open for 12% of the time, Pallas kernels for 0%

commit v1 on v0

--- a/solution.py
+++ b/solution.py
@@ -3,6 +3,7 @@
 import jax.numpy as jnp
 from jax import lax
 from jax.sharding import PartitionSpec as P
+from jax.lax import axis_index, axis_size, ppermute
 
 HEAD_DIM = 128
 TOPK = 4
@@ -11,6 +12,21 @@
 CAP = 160
 epsilon = 1e-05
 highest = lax.Precision.HIGHEST
+
+
+def search_cycles(array_in, a_name):
+    workers = axis_size(a_name)
+    runs = tuple(((ix, (ix + 1) % workers) for ix in range(workers)))
+    kept_rows = tuple(((ix, (ix - 1) % workers) for ix in range(workers)))
+    u1, block_now = ([array_in], [array_in])
+    for _ in range(workers // 2):
+        u1.append(ppermute(u1[-1], a_name, runs))
+    j = 0
+    while j < (workers - 1) // 2:
+        block_now.append(ppermute(block_now[-1], a_name, kept_rows))
+        j = j + 1
+    block_last = jnp.concatenate([*u1[::-1], *block_now[1:]], axis=0)
+    return jnp.roll(block_last, (axis_index(a_name) - workers // 2) * array_in.shape[0], axis=0)
 
 
 def inv_rms(values):
@@ -77,7 +93,7 @@
     attn_gain_all, qkv_all, out_all, mlp_gain_all, router_all = (
         lax.all_gather(attn_gain, ("fsdp", "ctx"), axis=0, tiled=True),
         lax.all_gather(qkv_weight, ("fsdp", "ctx"), axis=0, tiled=True),
-        lax.all_gather(out_weight, ("fsdp", "ctx"), axis=0, tiled=True),
+        search_cycles(out_weight, ("fsdp", "ctx")),
         lax.all_gather(mlp_gain, ("fsdp", "ctx"), axis=0, tiled=True),
         lax.all_gather(router_weight, ("fsdp", "ctx"), axis=0, tiled=True),
     )

time: 2220 us -> 2200 us (level)
  waiting for transfers between devices: 1640 us -> 1580 us
    all_gather x1 -> x0, waiting for transfers between devices: 46.1 us -> none  [on_device(): lax.all_gather(out_weight, ('fsdp', 'ctx'), axis=0, tiled=True)]
    all_gather x1, waiting for transfers between devices: 78.4 us -> 41.3 us  [on_device(): lax.all_gather(qkv_weight, ('fsdp', 'ctx'), axis=0, tiled=True)]
    ppermute x0 -> x7, waiting for transfers between devices: none -> 33.4 us  [the longest x4 33.4 us: search_cycles(): u1.append(ppermute(u1[-1], a_name, runs))]
    unnamed x162 -> x203, local copies, waits for them, and re-layouts: 26.7 us -> 44.5 us
  transfers between devices with their start and end apart: 15 -> 21, of which waited for: 13 -> 15; matrix products, arithmetic and copies ran while one was open for 12% -> 14% of each run, Pallas kernels for 0% -> 0%
where the time goes in v1:
time: 2200 us; the launch traced here: 2190 us
  waiting for transfers between devices  1580 us (72%)
  other arithmetic  152 us (7%)
  blocking collectives  148 us (7%)
  matrix products  143 us (6%)
  local copies, waits for them, and re-layouts  124 us (6%)
  starting transfers between devices  22.5 us (1%)
    reduce_scatter x1, waiting for transfers between devices, on_device(): lax.psum_scatter(jnp.concatenate([gate_up_term, down_term[:, None]], axis...  749 us
    reduce_scatter x1, waiting for transfers between devices, on_device(): lax.psum_scatter(grad_qkv, ('fsdp', 'ctx'), scatter_dimension=0, tiled=True)  212 us
    all_gather x1, waiting for transfers between devices, on_device(): lax.all_gather(gate_up_weight, ('fsdp', 'ctx'), axis=0, tiled=True)  181 us
    all_gather x1, waiting for transfers between devices, on_device(): lax.all_gather(down_weight, ('fsdp', 'ctx'), axis=0, tiled=True)  114 us
    reduce_scatter x1, waiting for transfers between devices, on_device(): lax.psum_scatter(grad_out, ('fsdp', 'ctx'), scatter_dimension=0, tiled=True)  91.2 us
    reduce_scatter x1, waiting for transfers between devices, on_device(): lax.psum_scatter(grad_router, ('fsdp', 'ctx'), scatter_dimension=0, tiled...  50.4 us
    unnamed x203, local copies, waits for them, and re-layouts  44.5 us
    scatter-add x8, other arithmetic, expert_forward(): combined.at[expert_tokens].add(returned_rows * expert_gates[:, None])  44.4 us
  transfers between devices with their start and end apart: 21, of which 15 were waited for; matrix products, arithmetic and copies ran while one was open for 14% of the time, Pallas kernels for 0%

profile of v1, /device:TPU:0, one launch (start us, length us, event | category | flops | bytes accessed | tf_op | source)
XLA Modules:
  0.0 2186.8 jit_solution(3326291407101773893)
XLA Ops:
  21.5 16.7 collective-permute-done.1
  49.4 10.9 collective-permute-done.2
  67.1 20.5 all-gather
  90.1 41.3 %all-gather.8.cloned.1.call-done = bf16[2048,3,512]{2,0,1:T(8,128)(2,1)} async-done(((bf16[256,3,512]{2,0,1:T(8,128)(2,1)}), bf16[2048,3,512]{2,0,1:T(8,128)(2,1)}) %all-gather.8.cloned.1.call-update) | async-done | bytes 6291472 | tf_op jit(solution)/shard_map/all_gather | solution.py:95
  181.5 26.7 %all-gather.10.cloned.1.call-done = bf16[1,1024,4,128]{1,3,2,0:T(8,128)(2,1)} async-done(((bf16[1,256,4,128]{1,3,2,0:T(8,128)(2,1)}), bf16[1,1024,4,128]{1,3,2,0:T(8,128)(2,1)}) %all-gather.10.cloned.1.call-update) | async-done | bytes 1048592 | tf_op jit(solution)/shard_map/all_gather | solution.py:126
  230.6 18.8 all-gather.1
  262.8 30.9 %all_gather.33 = bf16[2048,8]{0,1:T(8,128)(2,1)S(1)} all-gather(bf16[256,8]{0,1:T(8,128)(2,1)S(1)} %copy-done.84), channel_id=1, replica_groups=mesh['fsdp'=2,'ctx'=4,'tp'=4] {'fsdp','ctx'}, dimensions={0}, use_global_device_ids=true | all-gather | bytes 36864 | tf_op jit(solution)/shard_map/all_gather | solution.py:98
  315.8 180.8 %all-gather.14.cloned.1.call-done = bf16[2048,2,8,256]{3,0,1,2:T(8,128)(2,1)} async-done(((bf16[256,2,8,256]{3,0,1,2:T(8,128)(2,1)}), bf16[2048,2,8,256]{3,0,1,2:T(8,128)(2,1)}) %all-gather.14.cloned.1.call-update) | async-done | bytes 16777232 | tf_op jit(solution)/shard_map/all_gather | solution.py:163
  496.6 11.8 fusion.16
  508.4 114.1 %all-gather.16.cloned.1.call-done = bf16[2048,8,256]{2,0,1:T(8,128)(2,1)} async-done(((bf16[256,8,256]{2,0,1:T(8,128)(2,1)}), bf16[2048,8,256]{2,0,1:T(8,128)(2,1)}) %all-gather.16.cloned.1.call-update) | async-done | bytes 8388624 | tf_op jit(solution)/shard_map/all_gather | solution.py:164
  622.5 10.0 fusion.58
  635.6 63.7 %while.29 = (s32[]{:T(128)}, f32[256,2048]{1,0:T(8,128)}, s32[8,160]{1,0:T(8,128)S(1)}, bf16[8,160,2,256]{3,1,2,0:T(8,128)(2,1)}, bf16[2048,2,8,256]{3,0,1,2:T(8,128)(2,1)}, /*index=5*/f32[8,160]{1,0:T(8,128)S(1)}, s32[]{:T(128)}) while((s32[]{:T(128)}, f32[256,2048]{1,0:T(8,128)}, s32[8,160]{1,0:T(8,128)S(1)}, ...), condition=%wide.region_24.25_spmd, body=%wide.region_22.24_spmd.sunk | while | flops 336200160 | bytes 7508829 | solution.py:232
  700.9 80.1 %while.28 = (s32[]{:T(128)}, f32[256,2048]{1,0:T(8,128)}, f32[8,160]{1,0:T(8,128)S(1)}, s32[8,160]{1,0:T(8,128)S(1)}, bf16[8,160,256]{2,1,0:T(8,128)(2,1)}, /*in...) while((s32[]{:T(128)}, f32[256,2048]{1,0:T(8,128)}, ...), condition=%wide.region_20.21_spmd, body=%wide.region_17.20_spmd.sunk | while | flops 169084224 | bytes 9793273 | solution.py:196
  787.5 25.6 %psum.75 = f32[256,4]{1,0:T(8,128)S(1)} all-reduce(f32[256,4]{1,0:T(8,128)S(1)} %reshape.775), channel_id=1, replica_groups=mesh['fsdp'=2,'ctx'=4,'tp'=4] {'tp'}, use_global_device_ids=true, to_apply=%region_26.27 | all-reduce | flops 1024 | bytes 8192 | tf_op jit(solution)/shard_map/psum | solution.py:249
  835.3 18.8 convolution_bitcast_fusion.1
  869.2 43.7 %reduce-scatter.7.cloned.1.call-done = f32[1,256,4,128]{3,1,2,0:T(8,128)} async-done(((f32[1,1024,4,128]{3,1,2,0:T(8,128)}), f32[1,256,4,128]{3,1,2,0:T(8,128)}) %reduce-scatter.7.cloned.1.call-update) | async-done | bytes 524304 | tf_op jit(solution)/shard_map/reduce_scatter | solution.py:299
  932.9 12.9 convolution_bitcast_fusion.2
  945.8 33.7 %pad_maximum_fusion = f32[2048,3,8,256]{0,3,1,2:T(8,128)} fusion(f32[2048,1,8,256]{0,3,1,2:T(8,128)} %convolution_bitcast_fusion.2, f32[2048,2,8,256]{0,3,1,2:T(8,128)} %convolution_bitcast_fusion.1), kind=kLoop, calls=%fused_computation.32 | loop fusion | flops 12582912 | bytes 100663296 | tf_op jit(solution)/shard_map/concatenate | solution.py:242
  997.3 19.3 all-reduce.14.cloned.1.call-done
  1018.7 38.9 %all-reduce.2 = (f32[2048]{0:T(1024)S(1)}, f32[2,512]{1,0:T(2,128)}, f32[2048]{0:T(1024)S(1)}) all-reduce(f32[2048]{0:T(1024)S(1)} %get-tuple-element.336, f32[2,512]{1,0:T(2,128)S(1)} %pad_maximum_fusion.6, f32[2048]{0:T(1024)S(1)} %get-tuple-element.334), channel_id=4, replica_groups=mesh['fsdp'=2,'ctx'=4,'tp'=4] {'fsdp','ctx'}, use_global_device_ids=true, to_apply=%region_40.41.clone | all-reduce | flops 5120 | bytes 40960
  1063.9 748.7 %reduce-scatter.17.cloned.1.call-done = f32[256,3,8,256]{0,3,1,2:T(8,128)} async-done(((f32[2048,3,8,256]{0,3,1,2:T(8,128)}), f32[256,3,8,256]{0,3,1,2:T(8,128)}) %reduce-scatter.17.cloned.1.call-update) | async-done | bytes 6291472 | tf_op jit(solution)/shard_map/reduce_scatter | solution.py:241
  1826.4 50.4 %reduce-scatter.15.cloned.1.call-done = f32[256,8]{0,1:T(8,128)} async-done(((f32[2048,8]{0,1:T(8,128)}), f32[256,8]{0,1:T(8,128)}) %reduce-scatter.15.cloned.1.call-update) | async-done | bytes 8208 | tf_op jit(solution)/shard_map/reduce_scatter | solution.py:337
  1876.8 91.2 %reduce-scatter.13.cloned.1.call-done = f32[256,512]{1,0:T(8,128)} async-done(((f32[2048,512]{1,0:T(8,128)}), f32[256,512]{1,0:T(8,128)}) %reduce-scatter.13.cloned.1.call-update) | async-done | bytes 524304 | tf_op jit(solution)/shard_map/reduce_scatter | solution.py:335
  1968.0 212.0 %reduce-scatter.11.cloned.1.call-done = f32[256,3,512]{2,0,1:T(8,128)} async-done(((f32[2048,3,512]{2,0,1:T(8,128)}), f32[256,3,512]{2,0,1:T(8,128)}) %reduce-scatter.11.cloned.1.call-update) | async-done | bytes 1572880 | tf_op jit(solution)/shard_map/reduce_scatter | solution.py:334
  (458 shorter events, 393.0 us)
Async XLA Ops:
  7.2 124.3 %copy-start.8 = (bf16[1,256,2048]{2,1,0:T(8,128)(2,1)S(1)}, bf16[1,256,2048]{2,1,0:T(8,128)(2,1)}, u32[]{:S(2)}) copy-start(bf16[1,256,2048]{2,1,0:T(8,128)(2,1)} %param.15) | copy-start | bytes 3145732
  7.2 124.2 %all-gather.8.cloned.1.call-start = ((), (), s32[]{:S(2)}) async-start(), calls=%async_computation.6 | async-start | bytes 7077888 | tf_op jit(solution)/shard_map/all_gather | solution.py:95
  7.9 168.4 %all-gather.12.cloned.1.call-start = ((), (), s32[]{:S(2)}) async-start(), calls=%async_computation.8 | async-start | bytes 1310720 | tf_op jit(solution)/shard_map/all_gather | solution.py:125
  8.0 13.4 collective-permute-start
  11.1 31.8 %collective-permute-start.4 = (bf16[256,512]{1,0:T(8,128)(2,1)}, bf16[256,512]{1,0:T(8,128)(2,1)S(1)}, u32[]{:S(2)}, u32[]{:S(2)}) collective-permute-start(bf16[256,512]{1,0:T(8,128)(2,1)} %param.18), channel_id=1, source_target_pairs={{0,28},{4,0},{8,4},{12,8},{16,12},{20,16},{24,20},{28,24},{1,29},{... | collective-permute-start | bytes 786440 | tf_op jit(solution)/shard_map/ppermute | solution.py:26
  21.4 110.0 %copy-start.41 = (bf16[256,512]{1,0:T(8,128)(2,1)}, bf16[256,512]{1,0:T(8,128)(2,1)S(1)}, u32[]{:S(2)}) copy-start(bf16[256,512]{1,0:T(8,128)(2,1)S(1)} %collective-permute-done) | copy-start | bytes 786436
  21.4 16.8 collective-permute-start.1
  38.2 22.0 %collective-permute-start.2 = (bf16[256,512]{1,0:T(8,128)(2,1)S(1)}, bf16[256,512]{1,0:T(8,128)(2,1)S(1)}, u32[]{:S(2)}, u32[]{:S(2)}) collective-permute-start(bf16[256,512]{1,0:T(8,128)(2,1)S(1)} %collective-permute-done.1), channel_id=1, source_target_pairs={{0,4},{4,8},{8,12},{12,16},{16,20},{20,24},{24,28},{28,0},{1,5},{5... | collective-permute-start | bytes 786440 | tf_op jit(solution)/shard_map/ppermute | solution.py:23
  42.2 104.2 %copy-start.27 = (f32[256,128]{1,0:T(8,128)}, f32[256,128]{1,0:T(8,128)S(1)}, u32[]{:S(2)}) copy-start(f32[256,128]{1,0:T(8,128)S(1)} %get-tuple-element.404) | copy-start | bytes 393220
  42.8 45.7 %collective-permute-start.5 = (bf16[256,512]{1,0:T(8,128)(2,1)S(1)}, bf16[256,512]{1,0:T(8,128)(2,1)}, u32[]{:S(2)}, u32[]{:S(2)}) collective-permute-start(bf16[256,512]{1,0:T(8,128)(2,1)S(1)} %collective-permute-done.4), channel_id=1, source_target_pairs={{0,28},{4,0},{8,4},{12,8},{16,12},{20,16},{24,20},{28,24},{1,29},{... | collective-permute-start | bytes 786440 | tf_op jit(solution)/shard_map/ppermute | solution.py:26
  60.3 28.3 %collective-permute-start.3 = (bf16[256,512]{1,0:T(8,128)(2,1)S(1)}, bf16[256,512]{1,0:T(8,128)(2,1)S(1)}, u32[]{:S(2)}, u32[]{:S(2)}) collective-permute-start(bf16[256,512]{1,0:T(8,128)(2,1)S(1)} %collective-permute-done.2), channel_id=1, source_target_pairs={{0,4},{4,8},{8,12},{12,16},{16,20},{20,24},{24,28},{28,0},{1,5},{5... | collective-permute-start | bytes 786440 | tf_op jit(solution)/shard_map/ppermute | solution.py:23
  88.5 67.7 %collective-permute-start.6 = (bf16[256,512]{1,0:T(8,128)(2,1)}, bf16[256,512]{1,0:T(8,128)(2,1)}, u32[]{:S(2)}, u32[]{:S(2)}) collective-permute-start(bf16[256,512]{1,0:T(8,128)(2,1)} %collective-permute-done.5), channel_id=1, source_target_pairs={{0,28},{4,0},{8,4},{12,8},{16,12},{20,16},{24,20},{28,24},{1,29},{... | collective-permute-start | bytes 786440 | tf_op jit(solution)/shard_map/ppermute | solution.py:26
  147.5 60.7 %all-gather.10.cloned.1.call-start = ((), (), s32[]{:S(2)}) async-start(), calls=%async_computation.7 | async-start | bytes 1310720 | tf_op jit(solution)/shard_map/all_gather | solution.py:126
  166.7 127.6 %all-reduce.10.cloned.1.call-start = ((), (), s32[]{:S(2)}) async-start(), calls=%async_computation.9 | async-start | bytes 4194304 | tf_op jit(solution)/shard_map/psum | solution.py:148
  216.1 280.4 %all-gather.14.cloned.1.call-start = ((), (), s32[]{:S(2)}) async-start(), calls=%async_computation.10 | async-start | bytes 18874368 | tf_op jit(solution)/shard_map/all_gather | solution.py:163
  219.8 402.7 %all-gather.16.cloned.1.call-start = ((), (), s32[]{:S(2)}) async-start(), calls=%async_computation.11 | async-start | bytes 9437184 | tf_op jit(solution)/shard_map/all_gather | solution.py:164
  222.2 591.1 %all-reduce.12.cloned.1.call-start = ((), (), s32[]{:S(2)}) async-start(), calls=%async_computation.12 | async-start | bytes 4194304 | tf_op jit(solution)/shard_map/psum | solution.py:249
  699.3 167.9 %reduce-scatter.9.cloned.1.call-start = ((), (), s32[]{:S(2)}) async-start(), calls=%async_computation.14 | async-start | bytes 2621440 | tf_op jit(solution)/shard_map/reduce_scatter | solution.py:300
  825.6 87.3 %reduce-scatter.7.cloned.1.call-start = ((), (), s32[]{:S(2)}) async-start(), calls=%async_computation.13 | async-start | bytes 2621440 | tf_op jit(solution)/shard_map/reduce_scatter | solution.py:299
  834.1 182.5 %all-reduce.14.cloned.1.call-start = ((), (), s32[]{:S(2)}) async-start(), calls=%async_computation.19 | async-start | bytes 8388608 | tf_op jit(solution)/shard_map/psum | solution.py:203
  931.8 880.7 %reduce-scatter.17.cloned.1.call-start = ((), (), s32[]{:S(2)}) async-start(), calls=%async_computation.18 | async-start | bytes 56623104 | tf_op jit(solution)/shard_map/reduce_scatter | solution.py:241
  979.6 897.2 %reduce-scatter.15.cloned.1.call-start = ((), (), s32[]{:S(2)}) async-start(), calls=%async_computation.17 | async-start | bytes 73728 | tf_op jit(solution)/shard_map/reduce_scatter | solution.py:337
  982.1 985.9 %reduce-scatter.13.cloned.1.call-start = ((), (), s32[]{:S(2)}) async-start(), calls=%async_computation.16 | async-start | bytes 4718592 | tf_op jit(solution)/shard_map/reduce_scatter | solution.py:335
  986.7 1193.2 %reduce-scatter.11.cloned.1.call-start = ((), (), s32[]{:S(2)}) async-start(), calls=%async_computation.15 | async-start | bytes 14155776 | tf_op jit(solution)/shard_map/reduce_scatter | solution.py:334
  (86 other events, 1656.6 us)
Sparse Core Ops, SparseCore 0:
  10.2 121.2 all-gather.7
  147.6 28.7 all-gather.11
  178.5 29.6 all-gather.9
  216.3 49.6 all-reduce.9
  268.8 227.7 all-gather.13
  499.4 123.1 all-gather.15
  699.5 49.5 all-reduce.11
  825.7 41.5 reduce-scatter.8
  869.7 43.1 reduce-scatter.6
  932.0 84.5 all-reduce.13
  1021.0 791.5 reduce-scatter.16
  1816.4 60.3 reduce-scatter.14
  1881.0 86.9 reduce-scatter.12
  1972.4 207.4 reduce-scatter.10
